TPU v7x, 32 devices: a whole 2x2x4 slice. The times are simulated.
32 devices in a mesh: pages: 16 (over z, x, core), tok: 2 (over y).
Axes of the slice: x: 2, y: 2, z: 4, core: 2. Of those that a mesh axis runs over, the one named last changes fastest.
Arguments:
- queries: bfloat16 [32, 32, 128], P('pages'), may hold values from -50 to 50
- pages: bfloat16 [16, 1024, 128], P('pages', 'tok'), may hold values from -10 to 10
- pad_counts: int32 [16], P('pages'), may hold values from 0 to 511
- labels: int32 [32, 16], P(None, 'pages'), may hold values 0 or 1
Outputs:
- query_grad: float32 [32, 32, 128], P('pages')
- page_grad: float32 [16, 1024, 128], P('pages', 'tok')
- page_loss: float32 [16], P('pages')
All inputs are finite; a program needn't handle non-finite values. No bound on the sum of `labels` on one device may be relied on, other than what follows from the above.
Results may differ from a plain program's by a relative error of at most 0.0025.
Values may be sent and summed in bfloat16 or wider, within the bound.
No kernel may reach another device: no remote copies, remote signals or barrier semaphores. Data moves between devices by JAX's collectives and lax.ppermute only.
A program may use at most 64 MiB of HBM per device.

v0:
```python
import math
import jax
import jax.numpy as jnp
from jax import lax
from jax.sharding import PartitionSpec as P

LP = 1024
MASKED = -1000000000.0
LOGIT_SPAN = 8.0
CENTRE_SHIFT = 0.5
FILL_SHARE = 0.75


def combined_all(value, axis, combine):
    everything = lax.all_gather(value, axis)
    first = everything[0]

    def lap(k, so_far):
        return combine(so_far, everything[k])

    return lax.fori_loop(1, lax.axis_size(axis), lap, first)


def combine_smooth(former, latter):
    highest = jnp.maximum(former, latter)
    return highest + jnp.log(jnp.exp(former - highest) + jnp.exp(latter - highest))


def on_device(queries, pages, pad_counts, labels):
    query_count, query_len, feature_width = queries.shape
    local_pages, local_tokens, _ = pages.shape
    score_scale = feature_width ** (-0.5)
    token_offset = lax.axis_index("tok") * local_tokens
    positions = token_offset + jnp.arange(local_tokens, dtype=jnp.int32)
    usable = positions[None, :] < (LP - pad_counts)[:, None]
    gathered = lax.all_gather(queries, "pages", axis=0, tiled=True)
    query_total = gathered.shape[0]
    row_count = query_total * query_len
    query_rows = gathered.reshape(row_count, feature_width)
    block_rows = math.gcd(row_count, 512)
    block_count = row_count // block_rows

    def scores_for(query_block, page_no):
        raw = (
            lax.dot_general(
                query_block,
                pages[page_no],
                (((1,), (1,)), ((), ())),
                preferred_element_type=jnp.float32,
            )
            * score_scale
        )
        return jnp.where(usable[page_no][None, :], raw, MASKED)

    def forward_block(block_index, running):
        offset = block_index * block_rows
        query_block = lax.dynamic_slice_in_dim(query_rows, offset, block_rows, 0)
        scores = scores_for(query_block, 0)
        highest = jnp.max(scores, axis=1)
        columns = [highest + jnp.log(jnp.sum(jnp.exp(scores - highest[:, None]), axis=1))]
        partial_value = jnp.stack(columns, axis=1)
        return lax.dynamic_update_slice_in_dim(running, partial_value, offset, 0)

    buffered = lax.fori_loop(
        0, block_count, forward_block, jnp.zeros((row_count, local_pages), jnp.float32)
    )
    smooth = combined_all(buffered, "tok", combine_smooth)
    similarity = smooth.reshape(query_total, query_len, local_pages).sum(axis=1)
    label_sign = 2.0 * labels.astype(jnp.float32) - 1.0
    logit_gain = LOGIT_SPAN / query_len
    centre = query_len * (CENTRE_SHIFT + math.log(FILL_SHARE * LP))
    logits = logit_gain * (similarity - centre)
    page_loss = jnp.sum(jax.nn.softplus(-label_sign * logits), axis=0)
    slope = logit_gain * (-label_sign * jax.nn.sigmoid(-label_sign * logits))
    row_slope = jnp.repeat(slope, query_len, axis=0)

    def backward_block(block_index, running):
        query_terms, page_terms = running
        offset = block_index * block_rows
        query_block = lax.dynamic_slice_in_dim(query_rows, offset, block_rows, 0)
        smooth_block = lax.dynamic_slice_in_dim(smooth, offset, block_rows, 0)
        slope_block = lax.dynamic_slice_in_dim(row_slope, offset, block_rows, 0)
        scores = scores_for(query_block, 0)
        weights = jnp.where(usable[0][None, :], jnp.exp(scores - smooth_block[:, 0][:, None]), 0.0)
        scaled = (weights * slope_block[:, 0][:, None]).astype(jnp.bfloat16)
        summed = jnp.dot(scaled, pages[0], preferred_element_type=jnp.float32)
        gradients = [
            lax.dot_general(
                scaled, query_block, (((0,), (0,)), ((), ())), preferred_element_type=jnp.float32
            )
        ]
        page_terms = page_terms + jnp.stack(gradients, axis=0)
        query_terms = lax.dynamic_update_slice_in_dim(query_terms, summed * score_scale, offset, 0)
        return (query_terms, page_terms)

    start_terms = (
        jnp.zeros((row_count, feature_width), jnp.float32),
        jnp.zeros((local_pages, local_tokens, feature_width), jnp.float32),
    )
    query_terms, page_terms = lax.fori_loop(0, block_count, backward_block, start_terms)
    page_grad = page_terms * score_scale
    owned = lax.psum_scatter(query_terms, "pages", scatter_dimension=0, tiled=True)
    owned = lax.psum(owned, "tok")
    query_grad = owned.reshape(query_count, query_len, feature_width)
    return (query_grad, page_grad, page_loss)


def solution(mesh):
    return jax.shard_map(
        on_device,
        mesh=mesh,
        in_specs=(P("pages", None, None), P("pages", "tok", None), P("pages"), P(None, "pages")),
        out_specs=(P("pages", None, None), P("pages", "tok", None), P("pages")),
        check_vma=False,
    )
```

profile of v0, /device:TPU:0, one launch (start us, length us, event | category | flops | bytes accessed | tf_op | source)
XLA Modules:
  0.0 112.6 jit_solution(9280587860546555923)
XLA Ops:
  7.2 0.0 reduce-scatter.2.cloned.1.call-start
  7.9 0.0 copy-start
  7.9 24.2 %all_gather.9 = bf16[32,32,128]{2,1,0:T(8,128)(2,1)S(1)} all-gather(bf16[2,32,128]{2,1,0:T(8,128)(2,1)} %param.8), channel_id=1, replica_groups=mesh['pages'=16,'tok'=2] {'pages'}, dimensions={0}, use_global_device_ids=true | all-gather | bytes 278528 | tf_op jit(solution)/shard_map/all_gather | solution.py:36
  32.1 0.0 copy-done
  32.1 1.2 %while.35 = (s32[]{:T(128)}, f32[1024,1]{0,1:T(1,128)S(1)}, bf16[1024,128]{1,0:T(8,128)(2,1)S(1)}, bf16[1,512,128]{2,1,0:T(8,128)(2,1)S(1)}, s32[]{:T(128)}, /*i...) while((s32[]{:T(128)}, f32[1024,1]{0,1:T(1,128)S(1)}, ...), condition=%wide.region_3.4_spmd.clone, body=%wide.region_0.3_spmd.clone.sunk | while | flops 68420104 | bytes 2376867 | solution.py:64
  32.1 0.3 fusion.38
  32.4 0.2 exponential_reduce_fusion.2
  32.7 0.3 fusion.38
  33.0 0.2 exponential_reduce_fusion.2
  33.2 4.4 %all-gather = f32[2048,1]{0,1:T(1,128)S(1)} all-gather(f32[1024,1]{0,1:T(1,128)S(1)} %get-tuple-element.249), channel_id=2, replica_groups=mesh['pages'=16,'tok'=2] {'tok'}, dimensions={0}, use_global_device_ids=true | all-gather | bytes 12288 | tf_op jit(solution)/shard_map/all_gather | solution.py:15
  37.6 0.1 squeeze.28
  37.7 0.1 squeeze.29
  37.8 0.0 copy-start.2
  37.8 0.1 add_reduce_fusion
  37.9 0.5 copy-done.2
  38.4 0.6 fusion.24
  39.1 0.1 broadcast_in_dim.84
  39.2 0.1 broadcast_in_dim.85
  39.3 2.4 %while.36 = (s32[]{:T(128)}, f32[1024,128]{1,0:T(8,128)S(1)}, f32[1,512,128]{2,1,0:T(8,128)S(1)}, bf16[1024,128]{1,0:T(8,128)(2,1)S(1)}, bf16[1,512,128]{2,1,0:T...) while((s32[]{:T(128)}, f32[1024,128]{1,0:T(8,128)S(1)}, ...), condition=%wide.region_6.7_spmd.clone, body=%wide.region_5.6_spmd.clone.sunk | while | flops 203097088 | bytes 2897109 | solution.py:100
  39.4 0.4 fusion.45
  39.8 0.4 fusion.47
  40.2 0.3 fusion.46
  40.5 0.4 fusion.45
  41.0 0.4 fusion.47
  41.4 0.3 fusion.46
  41.7 0.0 copy-start.1
  41.7 0.8 copy-done.1
  42.5 0.0 reduce-scatter.2.cloned.1.call-update
  42.5 0.7 broadcast_multiply_fusion
  43.2 52.9 %reduce-scatter.2.cloned.1.call-done = f32[64,128]{1,0:T(8,128)} async-done(((f32[1024,128]{1,0:T(8,128)}), f32[64,128]{1,0:T(8,128)}) %reduce-scatter.2.cloned.1.call-update) | async-done | bytes 32784 | tf_op jit(solution)/shard_map/reduce_scatter | solution.py:102
  96.2 9.6 %psum.7 = f32[2,32,128]{2,1,0:T(8,128)} all-reduce(f32[2,32,128]{2,1,0:T(8,128)} %bitcast.50), channel_id=1, replica_groups=mesh['pages'=16,'tok'=2] {'tok'}, use_global_device_ids=true, to_apply=%region_8.9 | all-reduce | flops 8192 | bytes 65536 | tf_op jit(solution)/shard_map/psum | solution.py:103
  (15 shorter events, 0.3 us)
Async XLA Ops:
  7.2 89.0 %reduce-scatter.2.cloned.1.call-start = ((), (), s32[]{:S(2)}) async-start(), calls=%async_computation.1 | async-start | bytes 557056 | tf_op jit(solution)/shard_map/reduce_scatter | solution.py:102
  7.9 24.2 %copy-start = (bf16[1,512,128]{2,1,0:T(8,128)(2,1)S(1)}, bf16[1,512,128]{2,1,0:T(8,128)(2,1)}, u32[]{:S(2)}) copy-start(bf16[1,512,128]{2,1,0:T(8,128)(2,1)} %param.9) | copy-start | bytes 393220
  37.8 0.7 copy-start.2
  41.7 0.8 copy-start.1
Sparse Core Ops, SparseCore 0:
  42.6 53.4 reduce-scatter.1
where the time goes:
time: 113 us
  waiting for transfers between devices  52.9 us (47%)
  blocking collectives  38.1 us (34%)
  between operations  14.7 us (13%)
  matrix products  2.87 us (3%)
  other arithmetic  2.05 us (2%)
  local copies, waits for them, and re-layouts  1.7 us (2%)
    reduce_scatter x1, waiting for transfers between devices, on_device(): lax.psum_scatter(query_terms, 'pages', scatter_dimension=0, tiled=True)  52.9 us
    all_gather x1, blocking collectives, on_device(): gathered = lax.all_gather(queries, 'pages', axis=0, tiled=True)  24.2 us
    psum x1, blocking collectives, on_device(): owned = lax.psum(owned, 'tok')  9.55 us
    all_gather x1, blocking collectives, combined_all(): everything = lax.all_gather(value, axis)  4.36 us
  transfers between devices with their start and end apart: 1, of which 1 were waited for; matrix products, arithmetic and copies ran while one was open for 1% of the time, Pallas kernels for 0%

commit v1 on v0

--- a/solution.py
+++ b/solution.py
@@ -100,7 +100,7 @@
     query_terms, page_terms = lax.fori_loop(0, block_count, backward_block, start_terms)
     page_grad = page_terms * score_scale
     owned = lax.psum_scatter(query_terms, "pages", scatter_dimension=0, tiled=True)
-    owned = lax.psum(owned, "tok")
+    owned = jnp.sum(lax.all_gather(owned, "tok"), axis=0)
     query_grad = owned.reshape(query_count, query_len, feature_width)
     return (query_grad, page_grad, page_loss)
 

time: 113 us -> 109 us (0.965)
  blocking collectives: 38.1 us -> 33.3 us
    psum x1 -> x0, blocking collectives: 9.55 us -> none  [on_device(): owned = lax.psum(owned, 'tok')]
    all_gather x0 -> x1, blocking collectives: none -> 4.78 us  [on_device(): owned = jnp.sum(lax.all_gather(owned, 'tok'), axis=0)]
where the time goes in v1:
time: 109 us; the launch traced here: 108 us
  waiting for transfers between devices  52.9 us (49%)
  blocking collectives  33.3 us (31%)
  between operations  14.7 us (13%)
  matrix products  2.89 us (3%)
  other arithmetic  2.67 us (2%)
  local copies, waits for them, and re-layouts  1.7 us (2%)
    reduce_scatter x1, waiting for transfers between devices, on_device(): lax.psum_scatter(query_terms, 'pages', scatter_dimension=0, tiled=True)  52.9 us
    all_gather x1, blocking collectives, on_device(): gathered = lax.all_gather(queries, 'pages', axis=0, tiled=True)  24.2 us
    all_gather x1, blocking collectives, on_device(): owned = jnp.sum(lax.all_gather(owned, 'tok'), axis=0)  4.78 us
    all_gather x1, blocking collectives, combined_all(): everything = lax.all_gather(value, axis)  4.36 us
  transfers between devices with their start and end apart: 1, of which 1 were waited for; matrix products, arithmetic and copies ran while one was open for 1% of the time, Pallas kernels for 0%

profile of v1, /device:TPU:0, one launch (start us, length us, event | category | flops | bytes accessed | tf_op | source)
XLA Modules:
  0.0 108.4 jit_solution(3898924558347769598)
XLA Ops:
  7.2 0.0 reduce-scatter.2.cloned.1.call-start
  7.9 0.0 copy-start
  7.9 24.2 %all_gather.15 = bf16[32,32,128]{2,1,0:T(8,128)(2,1)S(1)} all-gather(bf16[2,32,128]{2,1,0:T(8,128)(2,1)} %param.8), channel_id=1, replica_groups=mesh['pages'=16,'tok'=2] {'pages'}, dimensions={0}, use_global_device_ids=true | all-gather | bytes 278528 | tf_op jit(solution)/shard_map/all_gather | solution.py:36
  32.1 0.0 copy-done
  32.1 1.2 %while.35 = (s32[]{:T(128)}, f32[1024,1]{0,1:T(1,128)S(1)}, bf16[1024,128]{1,0:T(8,128)(2,1)S(1)}, bf16[1,512,128]{2,1,0:T(8,128)(2,1)S(1)}, s32[]{:T(128)}, /*i...) while((s32[]{:T(128)}, f32[1024,1]{0,1:T(1,128)S(1)}, ...), condition=%wide.region_3.4_spmd.clone, body=%wide.region_0.3_spmd.clone.sunk | while | flops 68420104 | bytes 2376867 | solution.py:64
  32.1 0.3 fusion.38
  32.4 0.2 exponential_reduce_fusion.2
  32.7 0.3 fusion.38
  33.0 0.2 exponential_reduce_fusion.2
  33.3 4.4 %all-gather = f32[2048,1]{0,1:T(1,128)S(1)} all-gather(f32[1024,1]{0,1:T(1,128)S(1)} %get-tuple-element.249), channel_id=2, replica_groups=mesh['pages'=16,'tok'=2] {'tok'}, dimensions={0}, use_global_device_ids=true | all-gather | bytes 12288 | tf_op jit(solution)/shard_map/all_gather | solution.py:15
  37.7 0.1 squeeze.28
  37.7 0.1 squeeze.29
  37.8 0.0 copy-start.2
  37.8 0.1 add_reduce_fusion
  37.9 0.5 copy-done.2
  38.5 0.6 fusion.24
  39.1 0.1 broadcast_in_dim.84
  39.2 0.1 broadcast_in_dim.85
  39.3 2.4 %while.36 = (s32[]{:T(128)}, f32[1024,128]{1,0:T(8,128)S(1)}, f32[1,512,128]{2,1,0:T(8,128)S(1)}, bf16[1024,128]{1,0:T(8,128)(2,1)S(1)}, bf16[1,512,128]{2,1,0:T...) while((s32[]{:T(128)}, f32[1024,128]{1,0:T(8,128)S(1)}, ...), condition=%wide.region_6.7_spmd.clone, body=%wide.region_5.6_spmd.clone.sunk | while | flops 203097088 | bytes 2897109 | solution.py:100
  39.4 0.4 fusion.45
  39.8 0.4 fusion.47
  40.2 0.3 fusion.46
  40.6 0.4 fusion.45
  41.0 0.4 fusion.47
  41.4 0.3 fusion.46
  41.7 0.0 copy-start.1
  41.7 0.8 copy-done.1
  42.5 0.0 reduce-scatter.2.cloned.1.call-update
  42.5 0.7 broadcast_multiply_fusion
  43.2 52.9 %reduce-scatter.2.cloned.1.call-done = f32[64,128]{1,0:T(8,128)} async-done(((f32[1024,128]{1,0:T(8,128)}), f32[64,128]{1,0:T(8,128)}) %reduce-scatter.2.cloned.1.call-update) | async-done | bytes 32784 | tf_op jit(solution)/shard_map/reduce_scatter | solution.py:102
  96.1 4.8 %all-gather.1 = f32[128,128]{1,0:T(8,128)S(1)} all-gather(f32[64,128]{1,0:T(8,128)} %reduce-scatter.2.cloned.1.call-done), channel_id=3, replica_groups=mesh['pages'=16,'tok'=2] {'tok'}, dimensions={0}, use_global_device_ids=true | all-gather | bytes 98304 | tf_op jit(solution)/shard_map/all_gather | solution.py:103
  100.9 0.6 reduce_sum.43
  (15 shorter events, 0.3 us)
Async XLA Ops:
  7.2 89.0 %reduce-scatter.2.cloned.1.call-start = ((), (), s32[]{:S(2)}) async-start(), calls=%async_computation.1 | async-start | bytes 557056 | tf_op jit(solution)/shard_map/reduce_scatter | solution.py:102
  7.9 24.2 %copy-start = (bf16[1,512,128]{2,1,0:T(8,128)(2,1)S(1)}, bf16[1,512,128]{2,1,0:T(8,128)(2,1)}, u32[]{:S(2)}) copy-start(bf16[1,512,128]{2,1,0:T(8,128)(2,1)} %param.9) | copy-start | bytes 393220
  37.8 0.7 copy-start.2
  41.7 0.8 copy-start.1
Sparse Core Ops, SparseCore 0:
  42.6 53.4 reduce-scatter.1
